TPU v7x, 256 devices: a whole 4x4x8 slice. The times are simulated.
256 devices in a mesh: depth: 32 (over z, x_hi, core), shot: 8 (over y, x_lo).
Axes of the slice: x: 4 (x_hi: 2, x_lo: 2; x = x_hi * 2 + x_lo), y: 4, z: 8, core: 2. Of those that a mesh axis runs over, the one named last changes fastest.
Arguments:
- courant: float32 [512, 64, 128], P('depth'), may hold values from 0.04 to 0.2
- wave_before: float32 [8, 512, 64, 128], P('shot', 'depth'), may hold values from -10 to 10
- wave_current: float32 [8, 512, 64, 128], P('shot', 'depth'), may hold values from -10 to 10
- adjoint_after: float32 [8, 512, 64, 128], P('shot', 'depth'), may hold values from -10 to 10
- adjoint_current: float32 [8, 512, 64, 128], P('shot', 'depth'), may hold values from -10 to 10
- source_cell: int32 [8], P('shot'), may hold values from 0 to 4194303
- wavelet: float32 [8, 4], P('shot'), may hold values from -15 to 15
- receiver_cell: int32 [8, 256], P('shot'), may hold values from 0 to 4194303
- residual: float32 [8, 4, 256], P('shot'), may hold values from -12 to 12
- history: float32 [2, 5, 512, 64, 128], P(None, None, 'depth', 'shot'), may hold values from -23 to 23, as said below
Outputs:
- gradient: float32 [512, 64, 128], P('depth', 'shot')
- direction: float32 [512, 64, 128], P('depth', 'shot')
- courant_next: float32 [512, 64, 128], P('depth')
Inputs may be any that keep to these rules, and one draw needn't show every extreme that they name: In every pair the sum over all cells of history[0] times history[1] is positive.
All inputs are finite; a program needn't handle non-finite values.
Results may differ from a plain program's by a relative error of at most 0.00026.
Values sent between devices are 32-bit elements; how exact they have to be, the bound alone decides.
A program may use at most 128 MiB of HBM per device.

v0:
```python
import jax
import jax.numpy as jnp
from jax import lax
from jax.sharding import PartitionSpec as P

STEPS = 4
PAIRS = 5
coefficients = (-205.0 / 72.0, 8.0 / 5.0, -1.0 / 5.0, 8.0 / 315.0, -1.0 / 560.0)


def with_halo(cells, sides, width):
    for axis, dim in sides:
        count = lax.axis_size(axis)
        ends = count - 1
        head = lax.slice_in_dim(cells, 0, width, axis=dim)
        tail = lax.slice_in_dim(cells, cells.shape[dim] - width, cells.shape[dim], axis=dim)
        cells = jnp.concatenate(
            [
                lax.ppermute(tail, axis, [(i, (i + 1) % count) for i in range(ends)]),
                cells,
                lax.ppermute(head, axis, [((i + 1) % count, i) for i in range(ends)]),
            ],
            axis=dim,
        )
    return cells


def laplace_core(extended):
    interior = extended[4:-4]
    count_rows = interior.shape[0]
    width_x = interior.shape[1]
    width_y = interior.shape[2]
    padded = jnp.pad(interior, ((0, 0), (4, 4), (4, 4)))
    summed = 3.0 * coefficients[0] * interior
    for reach in range(1, 5):
        weight = coefficients[reach]
        summed = summed + weight * (
            extended[4 + reach : 4 + reach + count_rows]
            + extended[4 - reach : 4 - reach + count_rows]
        )
        summed = summed + weight * (
            padded[:, 4 + reach : 4 + reach + width_x, 4 : 4 + width_y]
            + padded[:, 4 - reach : 4 - reach + width_x, 4 : 4 + width_y]
        )
        summed = summed + weight * (
            padded[:, 4 : 4 + width_x, 4 + reach : 4 + reach + width_y]
            + padded[:, 4 : 4 + width_x, 4 - reach : 4 - reach + width_y]
        )
    return summed


def inject(volume, cell_ids, values, offset):
    count_rows = volume.shape[0]
    plane_size = volume.shape[1] * volume.shape[2]
    depth_row = cell_ids // plane_size - offset
    remainder = cell_ids % plane_size
    inside = (depth_row >= 0) & (depth_row < count_rows)
    row_safe = jnp.clip(depth_row, 0, count_rows - 1)
    return volume.at[row_safe, remainder // volume.shape[2], remainder % volume.shape[2]].add(
        jnp.where(inside, values, jnp.zeros_like(values))
    )


def per_device(
    courant,
    wave_before,
    wave_current,
    adjoint_after,
    adjoint_current,
    source_cell,
    wavelet,
    receiver_cell,
    residual,
    history,
):
    slab_rows = courant.shape[0]
    first_row = lax.axis_index("depth") * slab_rows
    shot_count = lax.axis_size("shot")
    summed = jnp.zeros(courant.shape, jnp.float32)
    laplacians = []
    wave_old = wave_before[0]
    wave_now = wave_current[0]
    for moment in range(STEPS):
        extended = with_halo(wave_now, (("depth", 0),), 4)
        laplacian = laplace_core(extended)
        wave_new = 2.0 * wave_now - wave_old + courant * laplacian
        wave_new = inject(wave_new, source_cell, wavelet[0, moment : moment + 1], first_row)
        laplacians.append(laplacian)
        wave_old, wave_now = (wave_now, wave_new)
    adjoint_old = adjoint_after[0]
    adjoint_now = adjoint_current[0]
    for moment in reversed(range(STEPS)):
        extended = with_halo(courant * adjoint_now, (("depth", 0),), 4)
        adjoint_new = 2.0 * adjoint_now - adjoint_old + laplace_core(extended)
        adjoint_new = inject(adjoint_new, receiver_cell[0], residual[0, moment], first_row)
        summed = summed + adjoint_new * laplacians[moment]
        adjoint_old, adjoint_now = (adjoint_now, adjoint_new)
    grad_piece = lax.psum_scatter(summed, "shot", scatter_dimension=1, tiled=True) * (
        1.0 / (shot_count * STEPS)
    )
    displaced = history[0]
    changes = history[1]
    step_change = jnp.einsum("izxy,jzxy->ij", displaced, changes, precision=lax.Precision.HIGHEST)
    change_change = jnp.einsum("izxy,jzxy->ij", changes, changes, precision=lax.Precision.HIGHEST)
    step_grad = jnp.sum(displaced * grad_piece, axis=(1, 2, 3))
    change_grad = jnp.sum(changes * grad_piece, axis=(1, 2, 3))
    packed = jnp.concatenate(
        [step_change, change_change, step_grad[None], change_grad[None]], axis=0
    )
    packed = lax.psum(packed, ("depth", "shot"))
    step_change = packed[:PAIRS]
    change_change = packed[PAIRS : 2 * PAIRS]
    step_grad = packed[2 * PAIRS]
    change_grad = packed[2 * PAIRS + 1]
    inverse = [1.0 / step_change[i, i] for i in range(PAIRS)]
    alphas = [None] * PAIRS
    for i in reversed(range(PAIRS)):
        value = step_grad[i]
        for j in range(i + 1, PAIRS):
            value = value - alphas[j] * step_change[i, j]
        alphas[i] = inverse[i] * value
    gamma = step_change[PAIRS - 1, PAIRS - 1] / change_change[PAIRS - 1, PAIRS - 1]
    gains = []
    for i in range(PAIRS):
        value = change_grad[i]
        for j in range(PAIRS):
            value = value - alphas[j] * change_change[i, j]
        value = gamma * value
        for j in range(i):
            value = value + gains[j] * step_change[j, i]
        gains.append(alphas[i] - inverse[i] * value)
    scaled = grad_piece
    for i in range(PAIRS):
        scaled = scaled - alphas[i] * changes[i]
    scaled = gamma * scaled
    for i in range(PAIRS):
        scaled = scaled + gains[i] * displaced[i]
    direction = -scaled
    piece_width = grad_piece.shape[1]
    own_courant = lax.dynamic_slice_in_dim(
        courant, lax.axis_index("shot") * piece_width, piece_width, 1
    )
    next_piece = own_courant + 0.05 * direction
    courant_next = lax.all_gather(next_piece, "shot", axis=1, tiled=True)
    return (grad_piece, direction, courant_next)


def solution(mesh):
    return jax.shard_map(
        per_device,
        mesh=mesh,
        in_specs=(
            P("depth", None, None),
            P("shot", "depth", None, None),
            P("shot", "depth", None, None),
            P("shot", "depth", None, None),
            P("shot", "depth", None, None),
            P("shot"),
            P("shot", None),
            P("shot", None),
            P("shot", None, None),
            P(None, None, "depth", "shot", None),
        ),
        out_specs=(P("depth", "shot", None), P("depth", "shot", None), P("depth", None, None)),
        check_vma=False,
    )
```

profile of v0, /device:TPU:32, one launch (start us, length us, event | category | flops | bytes accessed | tf_op | source)
XLA Modules:
  0.0 397.9 jit_solution(11437620847095359479)
XLA Ops:
  7.2 1.3 bitcast_multiply_fusion
  8.6 4.0 %collective-permute-start = (f32[4,64,128]{2,1,0:T(8,128)S(1)}, f32[4,64,128]{2,1,0:T(8,128)S(1)}, u32[]{:S(2)}, u32[]{:S(2)}) collective-permute-start(f32[4,64,128]{2,1,0:T(8,128)S(1)} %get-tuple-element.70), channel_id=1, source_target_pairs={{8,0},{16,8},{24,16},{32,24},{40,32},{48,40},{56,48},{64,56},{72,6... | collective-permute-start | bytes 393224 | tf_op jit(solution)/shard_map/ppermute | solution.py:21
  12.7 1.9 collective-permute-start.1
  14.7 6.0 %collective-permute-start.2 = (f32[4,64,128]{2,1,0:T(8,128)S(1)}, f32[4,64,128]{2,1,0:T(8,128)S(1)}, u32[]{:S(2)}, u32[]{:S(2)}) collective-permute-start(f32[4,64,128]{2,1,0:T(8,128)S(1)} %get-tuple-element.68), channel_id=1, source_target_pairs={{8,0},{16,8},{24,16},{32,24},{40,32},{48,40},{56,48},{64,56},{72,6... | collective-permute-start | bytes 393224 | tf_op jit(solution)/shard_map/ppermute | solution.py:21
  20.7 1.9 collective-permute-start.3
  23.3 0.7 fusion.369
  26.7 0.7 and_reduce_fusion
  27.4 1.9 fusion.184
  29.4 23.9 %scatter_fusion = f32[16,64,128]{2,1,0:T(8,128)S(1)} fusion(f32[16,64,128]{2,1,0:T(8,128)S(1)} %fusion.184, s32[256]{0:T(256)S(1)} %bitcast.180, f32[256]{0:T(256)} %get-tuple-element.128), kind=kCustom, calls=%fused_computation | custom fusion | flops 256 | bytes 6144 | tf_op jit(solution)/shard_map/scatter-add | solution.py:59
  53.4 3.7 fusion.348
  57.0 0.7 dynamic-slice.24
  59.8 6.1 %collective-permute-start.10 = (f32[4,64,128]{2,1,0:T(8,128)S(1)}, f32[4,64,128]{2,1,0:T(8,128)S(1)}, u32[]{:S(2)}, u32[]{:S(2)}) collective-permute-start(f32[4,64,128]{2,1,0:T(8,128)S(1)} %get-tuple-element.59), channel_id=1, source_target_pairs={{8,0},{16,8},{24,16},{32,24},{40,32},{48,40},{56,48},{64,56},{72,6... | collective-permute-start | bytes 393224 | tf_op jit(solution)/shard_map/ppermute | solution.py:21
  65.9 1.9 collective-permute-start.11
  67.8 0.7 fusion.363
  68.5 6.0 %collective-permute-start.4 = (f32[4,64,128]{2,1,0:T(8,128)}, f32[4,64,128]{2,1,0:T(8,128)S(1)}, u32[]{:S(2)}, u32[]{:S(2)}) collective-permute-start(f32[4,64,128]{2,1,0:T(8,128)} %get-tuple-element.66), channel_id=1, source_target_pairs={{8,0},{16,8},{24,16},{32,24},{40,32},{48,40},{56,48},{64,56},{72,6... | collective-permute-start | bytes 393224 | tf_op jit(solution)/shard_map/ppermute | solution.py:21
  74.5 1.9 collective-permute-start.5
  76.5 9.1 %fusion.59 = f32[16,64,128]{2,1,0:T(8,128)S(1)} fusion(f32[16,64,128]{2,1,0:T(8,128)} %copy-done.6, f32[4,64,128]{2,1,0:T(8,128)S(1)} %collective-permute-done.11, f32[4,64,128]{2,1,0:T(8,128)S(1)} %collective-permute-done.10, f32[1,16,64,128]{3,2,1,0:T(8,128)S(1)} %copy-done.2, f32[16,64,128]{2,1,0:T(8,128)S(1)} %scatter_fusion), kind=kLoop, calls=%fused_computation.289 | loop fusion | flops 6291456 | bytes 2359296 | tf_op jit(solution)/shard_map/add | solution.py:94
  85.6 15.2 %scatter_fusion.1 = f32[16,64,128]{2,1,0:T(8,128)S(1)} fusion(f32[16,64,128]{2,1,0:T(8,128)S(1)} %fusion.59, s32[256]{0:T(256)S(1)} %bitcast.181, f32[256]{0:T(256)S(1)} %get-tuple-element.127), kind=kCustom, calls=%fused_computation.1 | custom fusion | flops 256 | bytes 6144 | tf_op jit(solution)/shard_map/scatter-add | solution.py:59
  100.9 2.7 multiply_add_fusion.1
  103.6 6.1 %collective-permute-start.12 = (f32[4,64,128]{2,1,0:T(8,128)S(1)}, f32[4,64,128]{2,1,0:T(8,128)S(1)}, u32[]{:S(2)}, u32[]{:S(2)}) collective-permute-start(f32[4,64,128]{2,1,0:T(8,128)S(1)} %get-tuple-element.56), channel_id=1, source_target_pairs={{8,0},{16,8},{24,16},{32,24},{40,32},{48,40},{56,48},{64,56},{72,6... | collective-permute-start | bytes 393224 | tf_op jit(solution)/shard_map/ppermute | solution.py:21
  109.7 1.9 collective-permute-start.13
  111.6 0.6 dynamic-slice.25
  114.3 0.7 fusion.362
  115.0 6.0 %collective-permute-start.6 = (f32[4,64,128]{2,1,0:T(8,128)}, f32[4,64,128]{2,1,0:T(8,128)S(1)}, u32[]{:S(2)}, u32[]{:S(2)}) collective-permute-start(f32[4,64,128]{2,1,0:T(8,128)} %get-tuple-element.64), channel_id=1, source_target_pairs={{8,0},{16,8},{24,16},{32,24},{40,32},{48,40},{56,48},{64,56},{72,6... | collective-permute-start | bytes 393224 | tf_op jit(solution)/shard_map/ppermute | solution.py:21
  121.1 1.9 collective-permute-start.7
  123.0 2.0 fusion.34
  125.0 15.2 %scatter_fusion.2 = f32[16,64,128]{2,1,0:T(8,128)S(1)} fusion(f32[16,64,128]{2,1,0:T(8,128)S(1)} %fusion.34, s32[256]{0:T(256)S(1)} %bitcast.182, f32[256]{0:T(256)S(1)} %get-tuple-element.126), kind=kCustom, calls=%fused_computation.2 | custom fusion | flops 256 | bytes 6144 | tf_op jit(solution)/shard_map/scatter-add | solution.py:59
  140.2 10.6 %multiply_add_fusion = (f32[16,64,128]{2,1,0:T(8,128)S(1)}, f32[16,64,128]{2,1,0:T(8,128)}, f32[16,64,128]{2,1,0:T(8,128)S(1)}) fusion(f32[16,64,128]{2,1,0:T(8,128)S(1)} %copy-done, f32[16,64,128]{2,1,0:T(8,128)S(1)} %scatter-add.44, f32[16,64,128]{2,1,0:T(8,128)} %copy-done.3, f32[4,64,128]{2,1,0:T(8,128)} %collective-permute-done.7, ...), kind=kLoop, calls=%fused_computation.602 | loop fusion | flops 6553600 | bytes 3932160 | tf_op jit(solution)/shard_map/add | solution.py:86
  150.9 6.1 %collective-permute-start.14 = (f32[4,64,128]{2,1,0:T(8,128)S(1)}, f32[4,64,128]{2,1,0:T(8,128)S(1)}, u32[]{:S(2)}, u32[]{:S(2)}) collective-permute-start(f32[4,64,128]{2,1,0:T(8,128)S(1)} %get-tuple-element.53), channel_id=1, source_target_pairs={{8,0},{16,8},{24,16},{32,24},{40,32},{48,40},{56,48},{64,56},{72,6... | collective-permute-start | bytes 393224 | tf_op jit(solution)/shard_map/ppermute | solution.py:21
  156.9 2.1 collective-permute-start.15
  161.7 0.7 fusion.361
  162.4 6.0 %collective-permute-start.8 = (f32[4,64,128]{2,1,0:T(8,128)}, f32[4,64,128]{2,1,0:T(8,128)S(1)}, u32[]{:S(2)}, u32[]{:S(2)}) collective-permute-start(f32[4,64,128]{2,1,0:T(8,128)} %get-tuple-element.62), channel_id=1, source_target_pairs={{8,0},{16,8},{24,16},{32,24},{40,32},{48,40},{56,48},{64,56},{72,6... | collective-permute-start | bytes 393224 | tf_op jit(solution)/shard_map/ppermute | solution.py:21
  168.5 1.9 collective-permute-start.9
  170.4 2.2 fusion.9
  172.7 15.2 %scatter_fusion.3 = f32[16,64,128]{2,1,0:T(8,128)S(1)} fusion(f32[16,64,128]{2,1,0:T(8,128)S(1)} %fusion.9, s32[256]{0:T(256)S(1)} %bitcast.183, f32[256]{0:T(256)S(1)} %get-tuple-element.43), kind=kCustom, calls=%fused_computation.3 | custom fusion | flops 256 | bytes 6144 | tf_op jit(solution)/shard_map/scatter-add | solution.py:59
  187.9 3.9 fusion.87
  191.9 1.1 fusion.357
  193.0 1.2 convolution_bitcast_fusion
  194.2 1.4 convolution_bitcast_fusion.1
  195.6 48.2 %reduce-scatter.2.cloned.1.call-done = f32[16,8,128]{2,1,0:T(8,128)} async-done(((f32[16,64,128]{2,1,0:T(8,128)}), f32[16,8,128]{2,1,0:T(8,128)}) %reduce-scatter.2.cloned.1.call-update) | async-done | bytes 65552 | tf_op jit(solution)/shard_map/reduce_scatter | solution.py:98
  243.7 0.8 broadcast_multiply_fusion
  245.4 73.3 %psum.7 = f32[12,5]{0,1:T(8,128)S(1)} all-reduce(f32[12,5]{0,1:T(8,128)S(1)} %pad_maximum_fusion.16), channel_id=1, replica_groups=mesh['depth'=32,'shot'=8] {'depth','shot'}, use_global_device_ids=true, to_apply=%region_8.9 | all-reduce | flops 60 | bytes 480 | tf_op jit(solution)/shard_map/psum | solution.py:110
  318.8 0.7 fusion.366
  319.5 0.7 fusion.367
  320.2 0.7 fusion.365
  359.7 0.7 multiply_add_fusion.2
  360.4 29.8 %all_gather.3 = f32[16,64,128]{2,1,0:T(8,128)S(1)} all-gather(f32[16,8,128]{2,1,0:T(8,128)S(1)} %get-tuple-element.41), channel_id=1, replica_groups=mesh['depth'=32,'shot'=8] {'shot'}, dimensions={1}, use_global_device_ids=true | all-gather | bytes 589824 | tf_op jit(solution)/shard_map/all_gather | solution.py:144
  390.3 0.8 copy.49
  (70 shorter events, 2.7 us)
Async XLA Ops:
  7.2 236.6 %reduce-scatter.2.cloned.1.call-start = ((), (), s32[]{:S(2)}) async-start(), calls=%async_computation.1 | async-start | bytes 589824 | tf_op jit(solution)/shard_map/reduce_scatter | solution.py:98
  7.2 20.2 %copy-start.10 = (f32[1,16,64,128]{3,2,1,0:T(8,128)S(1)}, f32[1,16,64,128]{3,2,1,0:T(8,128)}, u32[]{:S(2)}) copy-start(f32[1,16,64,128]{3,2,1,0:T(8,128)} %param.19) | copy-start | bytes 1572868
  8.5 6.1 %copy-start.1 = (f32[1,16,64,128]{3,2,1,0:T(8,128)S(1)}, f32[1,16,64,128]{3,2,1,0:T(8,128)}, u32[]{:S(2)}) copy-start(f32[1,16,64,128]{3,2,1,0:T(8,128)} %param.18) | copy-start | bytes 1572868
  8.6 14.1 %copy-start.14 = (f32[1,4,256]{2,1,0:T(4,128)S(1)}, f32[1,4,256]{2,1,0:T(4,128)}, u32[]{:S(2)}) copy-start(f32[1,4,256]{2,1,0:T(4,128)} %param.24) | copy-start | bytes 12292
  8.6 14.1 %copy-start.15 = (s32[1,256]{1,0:T(1,128)S(1)}, s32[1,256]{1,0:T(1,128)}, u32[]{:S(2)}) copy-start(s32[1,256]{1,0:T(1,128)} %param.23) | copy-start | bytes 3076
  8.6 14.7 %copy-start.13 = (f32[1,4]{1,0:T(1,128)S(1)}, f32[1,4]{1,0:T(1,128)}, u32[]{:S(2)}) copy-start(f32[1,4]{1,0:T(1,128)} %param.22) | copy-start | bytes 52
  8.6 18.1 %copy-start.16 = (s32[3]{0:T(128)S(1)}, s32[3]{0:T(128)}, u32[]{:S(2)}) copy-start(s32[3]{0:T(128)} %constant.255.clone.1) | copy-start | bytes 40
  8.6 18.8 %copy-start.2 = (f32[1,16,64,128]{3,2,1,0:T(8,128)S(1)}, f32[1,16,64,128]{3,2,1,0:T(8,128)}, u32[]{:S(2)}) copy-start(f32[1,16,64,128]{3,2,1,0:T(8,128)} %param.20) | copy-start | bytes 1572868
  8.6 18.8 %collective-permute-start = (f32[4,64,128]{2,1,0:T(8,128)S(1)}, f32[4,64,128]{2,1,0:T(8,128)S(1)}, u32[]{:S(2)}, u32[]{:S(2)}) collective-permute-start(f32[4,64,128]{2,1,0:T(8,128)S(1)} %get-tuple-element.70), channel_id=1, source_target_pairs={{8,0},{16,8},{24,16},{32,24},{40,32},{48,40},{56,48},{64,56},{72,6... | collective-permute-start | bytes 393224 | tf_op jit(solution)/shard_map/ppermute | solution.py:21
  12.7 14.7 %collective-permute-start.1 = (f32[4,64,128]{2,1,0:T(8,128)S(1)}, f32[4,64,128]{2,1,0:T(8,128)S(1)}, u32[]{:S(2)}, u32[]{:S(2)}) collective-permute-start(f32[4,64,128]{2,1,0:T(8,128)S(1)} %get-tuple-element.71), channel_id=1, source_target_pairs={{0,8},{8,16},{16,24},{24,32},{32,40},{40,48},{48,56},{56,64},{64,7... | collective-permute-start | bytes 393224 | tf_op jit(solution)/shard_map/ppermute | solution.py:19
  14.7 38.7 %collective-permute-start.2 = (f32[4,64,128]{2,1,0:T(8,128)S(1)}, f32[4,64,128]{2,1,0:T(8,128)S(1)}, u32[]{:S(2)}, u32[]{:S(2)}) collective-permute-start(f32[4,64,128]{2,1,0:T(8,128)S(1)} %get-tuple-element.68), channel_id=1, source_target_pairs={{8,0},{16,8},{24,16},{32,24},{40,32},{48,40},{56,48},{64,56},{72,6... | collective-permute-start | bytes 393224 | tf_op jit(solution)/shard_map/ppermute | solution.py:21
  20.7 32.6 %collective-permute-start.3 = (f32[4,64,128]{2,1,0:T(8,128)S(1)}, f32[4,64,128]{2,1,0:T(8,128)S(1)}, u32[]{:S(2)}, u32[]{:S(2)}) collective-permute-start(f32[4,64,128]{2,1,0:T(8,128)S(1)} %get-tuple-element.69), channel_id=1, source_target_pairs={{0,8},{8,16},{16,24},{24,32},{32,40},{40,48},{48,56},{56,64},{64,7... | collective-permute-start | bytes 393224 | tf_op jit(solution)/shard_map/ppermute | solution.py:19
  29.4 24.0 %copy-start = (f32[16,64,128]{2,1,0:T(8,128)S(1)}, f32[16,64,128]{2,1,0:T(8,128)}, u32[]{:S(2)}) copy-start(f32[16,64,128]{2,1,0:T(8,128)} %param.16) | copy-start | bytes 1572868
  57.0 19.4 %copy-start.6 = (f32[16,64,128]{2,1,0:T(8,128)}, f32[16,64,128]{2,1,0:T(8,128)S(1)}, u32[]{:S(2)}) copy-start(f32[16,64,128]{2,1,0:T(8,128)S(1)} %get-tuple-element.61) | copy-start | bytes 1572868
  59.8 16.6 %collective-permute-start.10 = (f32[4,64,128]{2,1,0:T(8,128)S(1)}, f32[4,64,128]{2,1,0:T(8,128)S(1)}, u32[]{:S(2)}, u32[]{:S(2)}) collective-permute-start(f32[4,64,128]{2,1,0:T(8,128)S(1)} %get-tuple-element.59), channel_id=1, source_target_pairs={{8,0},{16,8},{24,16},{32,24},{40,32},{48,40},{56,48},{64,56},{72,6... | collective-permute-start | bytes 393224 | tf_op jit(solution)/shard_map/ppermute | solution.py:21
  65.9 10.6 %collective-permute-start.11 = (f32[4,64,128]{2,1,0:T(8,128)S(1)}, f32[4,64,128]{2,1,0:T(8,128)S(1)}, u32[]{:S(2)}, u32[]{:S(2)}) collective-permute-start(f32[4,64,128]{2,1,0:T(8,128)S(1)} %get-tuple-element.60), channel_id=1, source_target_pairs={{0,8},{8,16},{16,24},{24,32},{32,40},{40,48},{48,56},{56,64},{64,7... | collective-permute-start | bytes 393224 | tf_op jit(solution)/shard_map/ppermute | solution.py:19
  68.5 32.4 %collective-permute-start.4 = (f32[4,64,128]{2,1,0:T(8,128)}, f32[4,64,128]{2,1,0:T(8,128)S(1)}, u32[]{:S(2)}, u32[]{:S(2)}) collective-permute-start(f32[4,64,128]{2,1,0:T(8,128)} %get-tuple-element.66), channel_id=1, source_target_pairs={{8,0},{16,8},{24,16},{32,24},{40,32},{48,40},{56,48},{64,56},{72,6... | collective-permute-start | bytes 393224 | tf_op jit(solution)/shard_map/ppermute | solution.py:21
  74.5 26.3 %collective-permute-start.5 = (f32[4,64,128]{2,1,0:T(8,128)S(1)}, f32[4,64,128]{2,1,0:T(8,128)S(1)}, u32[]{:S(2)}, u32[]{:S(2)}) collective-permute-start(f32[4,64,128]{2,1,0:T(8,128)S(1)} %get-tuple-element.67), channel_id=1, source_target_pairs={{0,8},{8,16},{16,24},{24,32},{32,40},{40,48},{48,56},{56,64},{64,7... | collective-permute-start | bytes 393224 | tf_op jit(solution)/shard_map/ppermute | solution.py:19
  103.6 9.3 %copy-start.7 = (f32[16,64,128]{2,1,0:T(8,128)}, f32[16,64,128]{2,1,0:T(8,128)S(1)}, u32[]{:S(2)}) copy-start(f32[16,64,128]{2,1,0:T(8,128)S(1)} %get-tuple-element.58) | copy-start | bytes 1572868
  103.6 19.4 %collective-permute-start.12 = (f32[4,64,128]{2,1,0:T(8,128)S(1)}, f32[4,64,128]{2,1,0:T(8,128)S(1)}, u32[]{:S(2)}, u32[]{:S(2)}) collective-permute-start(f32[4,64,128]{2,1,0:T(8,128)S(1)} %get-tuple-element.56), channel_id=1, source_target_pairs={{8,0},{16,8},{24,16},{32,24},{40,32},{48,40},{56,48},{64,56},{72,6... | collective-permute-start | bytes 393224 | tf_op jit(solution)/shard_map/ppermute | solution.py:21
  109.7 13.3 %collective-permute-start.13 = (f32[4,64,128]{2,1,0:T(8,128)S(1)}, f32[4,64,128]{2,1,0:T(8,128)S(1)}, u32[]{:S(2)}, u32[]{:S(2)}) collective-permute-start(f32[4,64,128]{2,1,0:T(8,128)S(1)} %get-tuple-element.57), channel_id=1, source_target_pairs={{0,8},{8,16},{16,24},{24,32},{32,40},{40,48},{48,56},{56,64},{64,7... | collective-permute-start | bytes 393224 | tf_op jit(solution)/shard_map/ppermute | solution.py:19
  114.3 10.7 %copy-start.3 = (f32[16,64,128]{2,1,0:T(8,128)}, f32[16,64,128]{2,1,0:T(8,128)S(1)}, u32[]{:S(2)}) copy-start(f32[16,64,128]{2,1,0:T(8,128)S(1)} %scatter-add.45) | copy-start | bytes 1572868
  114.3 8.7 %copy-start.8 = (f32[16,64,128]{2,1,0:T(8,128)S(1)}, f32[16,64,128]{2,1,0:T(8,128)}, u32[]{:S(2)}) copy-start(f32[16,64,128]{2,1,0:T(8,128)} %copy-done.7) | copy-start | bytes 1572868
  115.0 25.2 %collective-permute-start.6 = (f32[4,64,128]{2,1,0:T(8,128)}, f32[4,64,128]{2,1,0:T(8,128)S(1)}, u32[]{:S(2)}, u32[]{:S(2)}) collective-permute-start(f32[4,64,128]{2,1,0:T(8,128)} %get-tuple-element.64), channel_id=1, source_target_pairs={{8,0},{16,8},{24,16},{32,24},{40,32},{48,40},{56,48},{64,56},{72,6... | collective-permute-start | bytes 393224 | tf_op jit(solution)/shard_map/ppermute | solution.py:21
  121.1 19.2 %collective-permute-start.7 = (f32[4,64,128]{2,1,0:T(8,128)}, f32[4,64,128]{2,1,0:T(8,128)}, u32[]{:S(2)}, u32[]{:S(2)}) collective-permute-start(f32[4,64,128]{2,1,0:T(8,128)} %get-tuple-element.65), channel_id=1, source_target_pairs={{0,8},{8,16},{16,24},{24,32},{32,40},{40,48},{48,56},{56,64},{64,7... | collective-permute-start | bytes 393224 | tf_op jit(solution)/shard_map/ppermute | solution.py:19
  150.8 9.5 %copy-start.4 = (f32[16,64,128]{2,1,0:T(8,128)}, f32[16,64,128]{2,1,0:T(8,128)S(1)}, u32[]{:S(2)}) copy-start(f32[16,64,128]{2,1,0:T(8,128)S(1)} %get-tuple-element.55) | copy-start | bytes 1572868
  150.9 19.6 %collective-permute-start.14 = (f32[4,64,128]{2,1,0:T(8,128)S(1)}, f32[4,64,128]{2,1,0:T(8,128)S(1)}, u32[]{:S(2)}, u32[]{:S(2)}) collective-permute-start(f32[4,64,128]{2,1,0:T(8,128)S(1)} %get-tuple-element.53), channel_id=1, source_target_pairs={{8,0},{16,8},{24,16},{32,24},{40,32},{48,40},{56,48},{64,56},{72,6... | collective-permute-start | bytes 393224 | tf_op jit(solution)/shard_map/ppermute | solution.py:21
  156.9 13.5 %collective-permute-start.15 = (f32[4,64,128]{2,1,0:T(8,128)S(1)}, f32[4,64,128]{2,1,0:T(8,128)}, u32[]{:S(2)}, u32[]{:S(2)}) collective-permute-start(f32[4,64,128]{2,1,0:T(8,128)S(1)} %get-tuple-element.54), channel_id=1, source_target_pairs={{0,8},{8,16},{16,24},{24,32},{32,40},{40,48},{48,56},{56,64},{64,7... | collective-permute-start | bytes 393224 | tf_op jit(solution)/shard_map/ppermute | solution.py:19
  161.7 8.7 %copy-start.5 = (f32[16,64,128]{2,1,0:T(8,128)S(1)}, f32[16,64,128]{2,1,0:T(8,128)}, u32[]{:S(2)}) copy-start(f32[16,64,128]{2,1,0:T(8,128)} %copy-done.4) | copy-start | bytes 1572868
  162.4 25.5 %collective-permute-start.8 = (f32[4,64,128]{2,1,0:T(8,128)}, f32[4,64,128]{2,1,0:T(8,128)S(1)}, u32[]{:S(2)}, u32[]{:S(2)}) collective-permute-start(f32[4,64,128]{2,1,0:T(8,128)} %get-tuple-element.62), channel_id=1, source_target_pairs={{8,0},{16,8},{24,16},{32,24},{40,32},{48,40},{56,48},{64,56},{72,6... | collective-permute-start | bytes 393224 | tf_op jit(solution)/shard_map/ppermute | solution.py:21
  168.5 19.4 %collective-permute-start.9 = (f32[4,64,128]{2,1,0:T(8,128)}, f32[4,64,128]{2,1,0:T(8,128)S(1)}, u32[]{:S(2)}, u32[]{:S(2)}) collective-permute-start(f32[4,64,128]{2,1,0:T(8,128)} %get-tuple-element.63), channel_id=1, source_target_pairs={{0,8},{8,16},{16,24},{24,32},{32,40},{40,48},{48,56},{56,64},{64,7... | collective-permute-start | bytes 393224 | tf_op jit(solution)/shard_map/ppermute | solution.py:19
  244.6 111.4 %copy-start.12 = (f32[16,8,128]{2,1,0:T(8,128)}, f32[16,8,128]{2,1,0:T(8,128)S(1)}, u32[]{:S(2)}) copy-start(f32[16,8,128]{2,1,0:T(8,128)S(1)} %broadcast_multiply_fusion) | copy-start | bytes 196612
  244.6 115.1 %copy-start.9 = (f32[2,5,16,8,128]{4,3,2,1,0:T(8,128)S(1)}, f32[2,5,16,8,128]{4,3,2,1,0:T(8,128)}, u32[]{:S(2)}) copy-start(f32[2,5,16,8,128]{4,3,2,1,0:T(8,128)} %param.25) | copy-start | bytes 1966084
  244.6 115.1 %copy-start.11 = (f32[16,8,128]{2,1,0:T(8,128)S(1)}, f32[16,8,128]{2,1,0:T(8,128)}, u32[]{:S(2)}) copy-start(f32[16,8,128]{2,1,0:T(8,128)} %reduce-scatter.2.cloned.1.call-done) | copy-start | bytes 196612
Sparse Core Ops, SparseCore 0:
  192.0 51.6 reduce-scatter.1
where the time goes:
time: 400 us; the launch traced here: 398 us
  other arithmetic  111 us (28%)
  blocking collectives  103 us (26%)
  starting transfers between devices  61.9 us (15%)
  between operations  61.9 us (15%)
  waiting for transfers between devices  48.2 us (12%)
  local copies, waits for them, and re-layouts  9.48 us (2%)
    psum x1, blocking collectives, per_device(): packed = lax.psum(packed, ('depth', 'shot'))  73.3 us
    scatter-add x4, other arithmetic, inject(): volume.at[row_safe, remainder // volume.shape[2], remainder % volume.shap...  69.6 us
    reduce_scatter x1, waiting for transfers between devices, per_device(): lax.psum_scatter(summed, 'shot', scatter_dimension=1, tiled=True)  48.2 us
    ppermute x8, starting transfers between devices, with_halo(): lax.ppermute(head, axis, [((i + 1) % count, i) for i in range(ends)])  46.4 us
    all_gather x1, blocking collectives, per_device(): courant_next = lax.all_gather(next_piece, 'shot', axis=1, tiled=True)  29.8 us
    add x3, other arithmetic, per_device(): wave_new = 2.0 * wave_now - wave_old + courant * laplacian  17 us
    ppermute x8, starting transfers between devices, with_halo(): lax.ppermute(tail, axis, [(i, (i + 1) % count) for i in range(ends)])  15.5 us
    add x4, other arithmetic, per_device(): adjoint_new = 2.0 * adjoint_now - adjoint_old + laplace_core(extended)  15.3 us
  transfers between devices with their start and end apart: 17, of which 1 were waited for; matrix products, arithmetic and copies ran while one was open for 24% of the time, Pallas kernels for 0%

commit v1 on v0

--- a/solution.py
+++ b/solution.py
@@ -141,7 +141,10 @@
         courant, lax.axis_index("shot") * piece_width, piece_width, 1
     )
     next_piece = own_courant + 0.05 * direction
-    courant_next = lax.all_gather(next_piece, "shot", axis=1, tiled=True)
+    size = lax.axis_size("shot")
+    parts = jnp.stack([next_piece for _ in range(size)])
+    parts = lax.all_to_all(parts, "shot", split_axis=0, concat_axis=0)
+    courant_next = jnp.concatenate(parts, axis=1)
     return (grad_piece, direction, courant_next)
 
 

time: 400 us -> 384 us (0.960)
  blocking collectives: 103 us -> 87.1 us
    all_gather x1 -> x0, blocking collectives: 29.8 us -> none  [per_device(): courant_next = lax.all_gather(next_piece, 'shot', axis=1, tiled=True)]
    all_to_all x0 -> x1, blocking collectives: none -> 13.7 us  [per_device(): parts = lax.all_to_all(parts, 'shot', split_axis=0, concat_axis=0)]
  transfers between devices with their start and end apart: 17 -> 17, of which waited for: 1 -> 1; matrix products, arithmetic and copies ran while one was open for 24% -> 25% of each run, Pallas kernels for 0% -> 0%
where the time goes in v1:
time: 384 us; the launch traced here: 382 us
  other arithmetic  111 us (29%)
  blocking collectives  87.1 us (23%)
  between operations  62 us (16%)
  starting transfers between devices  61.9 us (16%)
  waiting for transfers between devices  48.2 us (13%)
  local copies, waits for them, and re-layouts  9.57 us (2%)
    psum x1, blocking collectives, per_device(): packed = lax.psum(packed, ('depth', 'shot'))  73.3 us
    scatter-add x4, other arithmetic, inject(): volume.at[row_safe, remainder // volume.shape[2], remainder % volume.shap...  69.6 us
    reduce_scatter x1, waiting for transfers between devices, per_device(): lax.psum_scatter(summed, 'shot', scatter_dimension=1, tiled=True)  48.2 us
    ppermute x8, starting transfers between devices, with_halo(): lax.ppermute(head, axis, [((i + 1) % count, i) for i in range(ends)])  46.4 us
    add x3, other arithmetic, per_device(): wave_new = 2.0 * wave_now - wave_old + courant * laplacian  17 us
    ppermute x8, starting transfers between devices, with_halo(): lax.ppermute(tail, axis, [(i, (i + 1) % count) for i in range(ends)])  15.5 us
    add x4, other arithmetic, per_device(): adjoint_new = 2.0 * adjoint_now - adjoint_old + laplace_core(extended)  15.3 us
    all_to_all x1, blocking collectives, per_device(): parts = lax.all_to_all(parts, 'shot', split_axis=0, concat_axis=0)  13.7 us
  transfers between devices with their start and end apart: 17, of which 1 were waited for; matrix products, arithmetic and copies ran while one was open for 25% of the time, Pallas kernels for 0%

profile of v1, /device:TPU:32, one launch (start us, length us, event | category | flops | bytes accessed | tf_op | source)
XLA Modules:
  0.0 381.9 jit_solution(1393123424275851371)
XLA Ops:
  7.2 1.3 bitcast_multiply_fusion
  8.6 4.0 %collective-permute-start = (f32[4,64,128]{2,1,0:T(8,128)S(1)}, f32[4,64,128]{2,1,0:T(8,128)S(1)}, u32[]{:S(2)}, u32[]{:S(2)}) collective-permute-start(f32[4,64,128]{2,1,0:T(8,128)S(1)} %get-tuple-element.70), channel_id=1, source_target_pairs={{8,0},{16,8},{24,16},{32,24},{40,32},{48,40},{56,48},{64,56},{72,6... | collective-permute-start | bytes 393224 | tf_op jit(solution)/shard_map/ppermute | solution.py:21
  12.7 1.9 collective-permute-start.1
  14.7 6.0 %collective-permute-start.2 = (f32[4,64,128]{2,1,0:T(8,128)S(1)}, f32[4,64,128]{2,1,0:T(8,128)S(1)}, u32[]{:S(2)}, u32[]{:S(2)}) collective-permute-start(f32[4,64,128]{2,1,0:T(8,128)S(1)} %get-tuple-element.68), channel_id=1, source_target_pairs={{8,0},{16,8},{24,16},{32,24},{40,32},{48,40},{56,48},{64,56},{72,6... | collective-permute-start | bytes 393224 | tf_op jit(solution)/shard_map/ppermute | solution.py:21
  20.7 1.9 collective-permute-start.3
  23.3 0.7 fusion.369
  26.7 0.7 and_reduce_fusion
  27.4 1.9 fusion.184
  29.4 23.9 %scatter_fusion = f32[16,64,128]{2,1,0:T(8,128)S(1)} fusion(f32[16,64,128]{2,1,0:T(8,128)S(1)} %fusion.184, s32[256]{0:T(256)S(1)} %bitcast.185, f32[256]{0:T(256)} %get-tuple-element.128), kind=kCustom, calls=%fused_computation | custom fusion | flops 256 | bytes 6144 | tf_op jit(solution)/shard_map/scatter-add | solution.py:59
  53.4 3.7 fusion.348
  57.0 0.7 dynamic-slice.24
  59.8 6.1 %collective-permute-start.10 = (f32[4,64,128]{2,1,0:T(8,128)S(1)}, f32[4,64,128]{2,1,0:T(8,128)S(1)}, u32[]{:S(2)}, u32[]{:S(2)}) collective-permute-start(f32[4,64,128]{2,1,0:T(8,128)S(1)} %get-tuple-element.59), channel_id=1, source_target_pairs={{8,0},{16,8},{24,16},{32,24},{40,32},{48,40},{56,48},{64,56},{72,6... | collective-permute-start | bytes 393224 | tf_op jit(solution)/shard_map/ppermute | solution.py:21
  65.9 1.9 collective-permute-start.11
  67.8 0.7 fusion.363
  68.5 6.0 %collective-permute-start.4 = (f32[4,64,128]{2,1,0:T(8,128)}, f32[4,64,128]{2,1,0:T(8,128)S(1)}, u32[]{:S(2)}, u32[]{:S(2)}) collective-permute-start(f32[4,64,128]{2,1,0:T(8,128)} %get-tuple-element.66), channel_id=1, source_target_pairs={{8,0},{16,8},{24,16},{32,24},{40,32},{48,40},{56,48},{64,56},{72,6... | collective-permute-start | bytes 393224 | tf_op jit(solution)/shard_map/ppermute | solution.py:21
  74.5 1.9 collective-permute-start.5
  76.5 9.1 %fusion.59 = f32[16,64,128]{2,1,0:T(8,128)S(1)} fusion(f32[16,64,128]{2,1,0:T(8,128)} %copy-done.6, f32[4,64,128]{2,1,0:T(8,128)S(1)} %collective-permute-done.11, f32[4,64,128]{2,1,0:T(8,128)S(1)} %collective-permute-done.10, f32[1,16,64,128]{3,2,1,0:T(8,128)S(1)} %copy-done.2, f32[16,64,128]{2,1,0:T(8,128)S(1)} %scatter_fusion), kind=kLoop, calls=%fused_computation.289 | loop fusion | flops 6291456 | bytes 2359296 | tf_op jit(solution)/shard_map/add | solution.py:94
  85.6 15.2 %scatter_fusion.1 = f32[16,64,128]{2,1,0:T(8,128)S(1)} fusion(f32[16,64,128]{2,1,0:T(8,128)S(1)} %fusion.59, s32[256]{0:T(256)S(1)} %bitcast.186, f32[256]{0:T(256)S(1)} %get-tuple-element.127), kind=kCustom, calls=%fused_computation.1 | custom fusion | flops 256 | bytes 6144 | tf_op jit(solution)/shard_map/scatter-add | solution.py:59
  100.9 2.7 multiply_add_fusion.1
  103.6 6.1 %collective-permute-start.12 = (f32[4,64,128]{2,1,0:T(8,128)S(1)}, f32[4,64,128]{2,1,0:T(8,128)S(1)}, u32[]{:S(2)}, u32[]{:S(2)}) collective-permute-start(f32[4,64,128]{2,1,0:T(8,128)S(1)} %get-tuple-element.56), channel_id=1, source_target_pairs={{8,0},{16,8},{24,16},{32,24},{40,32},{48,40},{56,48},{64,56},{72,6... | collective-permute-start | bytes 393224 | tf_op jit(solution)/shard_map/ppermute | solution.py:21
  109.7 1.9 collective-permute-start.13
  111.6 0.6 dynamic-slice.25
  114.3 0.7 fusion.362
  115.0 6.0 %collective-permute-start.6 = (f32[4,64,128]{2,1,0:T(8,128)}, f32[4,64,128]{2,1,0:T(8,128)S(1)}, u32[]{:S(2)}, u32[]{:S(2)}) collective-permute-start(f32[4,64,128]{2,1,0:T(8,128)} %get-tuple-element.64), channel_id=1, source_target_pairs={{8,0},{16,8},{24,16},{32,24},{40,32},{48,40},{56,48},{64,56},{72,6... | collective-permute-start | bytes 393224 | tf_op jit(solution)/shard_map/ppermute | solution.py:21
  121.1 1.9 collective-permute-start.7
  123.0 2.0 fusion.34
  125.0 15.2 %scatter_fusion.2 = f32[16,64,128]{2,1,0:T(8,128)S(1)} fusion(f32[16,64,128]{2,1,0:T(8,128)S(1)} %fusion.34, s32[256]{0:T(256)S(1)} %bitcast.187, f32[256]{0:T(256)S(1)} %get-tuple-element.126), kind=kCustom, calls=%fused_computation.2 | custom fusion | flops 256 | bytes 6144 | tf_op jit(solution)/shard_map/scatter-add | solution.py:59
  140.2 10.6 %multiply_add_fusion = (f32[16,64,128]{2,1,0:T(8,128)S(1)}, f32[16,64,128]{2,1,0:T(8,128)}, f32[16,64,128]{2,1,0:T(8,128)S(1)}) fusion(f32[16,64,128]{2,1,0:T(8,128)S(1)} %copy-done, f32[16,64,128]{2,1,0:T(8,128)S(1)} %scatter-add.44, f32[16,64,128]{2,1,0:T(8,128)} %copy-done.3, f32[4,64,128]{2,1,0:T(8,128)} %collective-permute-done.7, ...), kind=kLoop, calls=%fused_computation.603 | loop fusion | flops 6553600 | bytes 3932160 | tf_op jit(solution)/shard_map/add | solution.py:86
  150.9 6.1 %collective-permute-start.14 = (f32[4,64,128]{2,1,0:T(8,128)S(1)}, f32[4,64,128]{2,1,0:T(8,128)S(1)}, u32[]{:S(2)}, u32[]{:S(2)}) collective-permute-start(f32[4,64,128]{2,1,0:T(8,128)S(1)} %get-tuple-element.53), channel_id=1, source_target_pairs={{8,0},{16,8},{24,16},{32,24},{40,32},{48,40},{56,48},{64,56},{72,6... | collective-permute-start | bytes 393224 | tf_op jit(solution)/shard_map/ppermute | solution.py:21
  156.9 2.1 collective-permute-start.15
  161.7 0.7 fusion.361
  162.4 6.0 %collective-permute-start.8 = (f32[4,64,128]{2,1,0:T(8,128)}, f32[4,64,128]{2,1,0:T(8,128)S(1)}, u32[]{:S(2)}, u32[]{:S(2)}) collective-permute-start(f32[4,64,128]{2,1,0:T(8,128)} %get-tuple-element.62), channel_id=1, source_target_pairs={{8,0},{16,8},{24,16},{32,24},{40,32},{48,40},{56,48},{64,56},{72,6... | collective-permute-start | bytes 393224 | tf_op jit(solution)/shard_map/ppermute | solution.py:21
  168.5 1.9 collective-permute-start.9
  170.4 2.2 fusion.9
  172.7 15.2 %scatter_fusion.3 = f32[16,64,128]{2,1,0:T(8,128)S(1)} fusion(f32[16,64,128]{2,1,0:T(8,128)S(1)} %fusion.9, s32[256]{0:T(256)S(1)} %bitcast.188, f32[256]{0:T(256)S(1)} %get-tuple-element.43), kind=kCustom, calls=%fused_computation.3 | custom fusion | flops 256 | bytes 6144 | tf_op jit(solution)/shard_map/scatter-add | solution.py:59
  187.9 3.9 %fusion.87 = f32[16,64,128]{2,1,0:T(8,128)} fusion(f32[16,64,128]{2,1,0:T(8,128)S(1)} %scatter_fusion, f32[16,64,128]{2,1,0:T(8,128)S(1)} %scatter-add.46, f32[4,64,128]{2,1,0:T(8,128)S(1)} %collective-permute-done.9, f32[4,64,128]{2,1,0:T(8,128)S(1)} %collective-permute-done.8, f32[16,64,128]{2,1,0:T(8,128)S(1)} %scatter_fusion.3, ...), kind=kLoop, calls=%fused_computation.317 | loop fusion | flops 6815744 | bytes 4980736 | tf_op jit(solution)/shard_map/add | solution.py:96
  191.9 1.1 fusion.357
  193.0 1.2 convolution_bitcast_fusion
  194.2 1.4 convolution_bitcast_fusion.1
  195.6 48.2 %reduce-scatter.2.cloned.1.call-done = f32[16,8,128]{2,1,0:T(8,128)} async-done(((f32[16,64,128]{2,1,0:T(8,128)}), f32[16,8,128]{2,1,0:T(8,128)}) %reduce-scatter.2.cloned.1.call-update) | async-done | bytes 65552 | tf_op jit(solution)/shard_map/reduce_scatter | solution.py:98
  243.7 0.8 broadcast_multiply_fusion
  245.4 73.3 %psum.7 = f32[12,5]{0,1:T(8,128)S(1)} all-reduce(f32[12,5]{0,1:T(8,128)S(1)} %pad_maximum_fusion.16), channel_id=1, replica_groups=mesh['depth'=32,'shot'=8] {'depth','shot'}, use_global_device_ids=true, to_apply=%region_8.9 | all-reduce | flops 60 | bytes 480 | tf_op jit(solution)/shard_map/psum | solution.py:110
  318.8 0.7 fusion.366
  319.5 0.7 fusion.367
  320.2 0.7 fusion.365
  359.7 0.7 multiply_add_fusion.2
  360.5 13.7 %all_to_all.5 = f32[8,16,8,128]{3,2,1,0:T(8,128)S(1)} all-to-all(f32[8,16,8,128]{3,2,1,0:T(8,128)S(1)} %stack.2), channel_id=1, replica_groups=mesh['depth'=32,'shot'=8] {'shot'}, dimensions={0} | all-to-all | bytes 1048576 | tf_op jit(solution)/shard_map/all_to_all | solution.py:146
  374.2 0.8 copy.52
  (71 shorter events, 2.8 us)
Async XLA Ops:
  7.2 236.6 %reduce-scatter.2.cloned.1.call-start = ((), (), s32[]{:S(2)}) async-start(), calls=%async_computation.2 | async-start | bytes 589824 | tf_op jit(solution)/shard_map/reduce_scatter | solution.py:98
  7.2 20.2 %copy-start.10 = (f32[1,16,64,128]{3,2,1,0:T(8,128)S(1)}, f32[1,16,64,128]{3,2,1,0:T(8,128)}, u32[]{:S(2)}) copy-start(f32[1,16,64,128]{3,2,1,0:T(8,128)} %param.19) | copy-start | bytes 1572868
  8.5 6.1 %copy-start.1 = (f32[1,16,64,128]{3,2,1,0:T(8,128)S(1)}, f32[1,16,64,128]{3,2,1,0:T(8,128)}, u32[]{:S(2)}) copy-start(f32[1,16,64,128]{3,2,1,0:T(8,128)} %param.18) | copy-start | bytes 1572868
  8.6 14.1 %copy-start.14 = (f32[1,4,256]{2,1,0:T(4,128)S(1)}, f32[1,4,256]{2,1,0:T(4,128)}, u32[]{:S(2)}) copy-start(f32[1,4,256]{2,1,0:T(4,128)} %param.24) | copy-start | bytes 12292
  8.6 14.1 %copy-start.15 = (s32[1,256]{1,0:T(1,128)S(1)}, s32[1,256]{1,0:T(1,128)}, u32[]{:S(2)}) copy-start(s32[1,256]{1,0:T(1,128)} %param.23) | copy-start | bytes 3076
  8.6 14.7 %copy-start.13 = (f32[1,4]{1,0:T(1,128)S(1)}, f32[1,4]{1,0:T(1,128)}, u32[]{:S(2)}) copy-start(f32[1,4]{1,0:T(1,128)} %param.22) | copy-start | bytes 52
  8.6 18.1 %copy-start.16 = (s32[3]{0:T(128)S(1)}, s32[3]{0:T(128)}, u32[]{:S(2)}) copy-start(s32[3]{0:T(128)} %constant.255.clone.1) | copy-start | bytes 40
  8.6 18.8 %copy-start.2 = (f32[1,16,64,128]{3,2,1,0:T(8,128)S(1)}, f32[1,16,64,128]{3,2,1,0:T(8,128)}, u32[]{:S(2)}) copy-start(f32[1,16,64,128]{3,2,1,0:T(8,128)} %param.20) | copy-start | bytes 1572868
  8.6 18.8 %collective-permute-start = (f32[4,64,128]{2,1,0:T(8,128)S(1)}, f32[4,64,128]{2,1,0:T(8,128)S(1)}, u32[]{:S(2)}, u32[]{:S(2)}) collective-permute-start(f32[4,64,128]{2,1,0:T(8,128)S(1)} %get-tuple-element.70), channel_id=1, source_target_pairs={{8,0},{16,8},{24,16},{32,24},{40,32},{48,40},{56,48},{64,56},{72,6... | collective-permute-start | bytes 393224 | tf_op jit(solution)/shard_map/ppermute | solution.py:21
  12.7 14.7 %collective-permute-start.1 = (f32[4,64,128]{2,1,0:T(8,128)S(1)}, f32[4,64,128]{2,1,0:T(8,128)S(1)}, u32[]{:S(2)}, u32[]{:S(2)}) collective-permute-start(f32[4,64,128]{2,1,0:T(8,128)S(1)} %get-tuple-element.71), channel_id=1, source_target_pairs={{0,8},{8,16},{16,24},{24,32},{32,40},{40,48},{48,56},{56,64},{64,7... | collective-permute-start | bytes 393224 | tf_op jit(solution)/shard_map/ppermute | solution.py:19
  14.7 38.7 %collective-permute-start.2 = (f32[4,64,128]{2,1,0:T(8,128)S(1)}, f32[4,64,128]{2,1,0:T(8,128)S(1)}, u32[]{:S(2)}, u32[]{:S(2)}) collective-permute-start(f32[4,64,128]{2,1,0:T(8,128)S(1)} %get-tuple-element.68), channel_id=1, source_target_pairs={{8,0},{16,8},{24,16},{32,24},{40,32},{48,40},{56,48},{64,56},{72,6... | collective-permute-start | bytes 393224 | tf_op jit(solution)/shard_map/ppermute | solution.py:21
  20.7 32.6 %collective-permute-start.3 = (f32[4,64,128]{2,1,0:T(8,128)S(1)}, f32[4,64,128]{2,1,0:T(8,128)S(1)}, u32[]{:S(2)}, u32[]{:S(2)}) collective-permute-start(f32[4,64,128]{2,1,0:T(8,128)S(1)} %get-tuple-element.69), channel_id=1, source_target_pairs={{0,8},{8,16},{16,24},{24,32},{32,40},{40,48},{48,56},{56,64},{64,7... | collective-permute-start | bytes 393224 | tf_op jit(solution)/shard_map/ppermute | solution.py:19
  29.4 24.0 %copy-start = (f32[16,64,128]{2,1,0:T(8,128)S(1)}, f32[16,64,128]{2,1,0:T(8,128)}, u32[]{:S(2)}) copy-start(f32[16,64,128]{2,1,0:T(8,128)} %param.16) | copy-start | bytes 1572868
  57.0 19.4 %copy-start.6 = (f32[16,64,128]{2,1,0:T(8,128)}, f32[16,64,128]{2,1,0:T(8,128)S(1)}, u32[]{:S(2)}) copy-start(f32[16,64,128]{2,1,0:T(8,128)S(1)} %get-tuple-element.61) | copy-start | bytes 1572868
  59.8 16.6 %collective-permute-start.10 = (f32[4,64,128]{2,1,0:T(8,128)S(1)}, f32[4,64,128]{2,1,0:T(8,128)S(1)}, u32[]{:S(2)}, u32[]{:S(2)}) collective-permute-start(f32[4,64,128]{2,1,0:T(8,128)S(1)} %get-tuple-element.59), channel_id=1, source_target_pairs={{8,0},{16,8},{24,16},{32,24},{40,32},{48,40},{56,48},{64,56},{72,6... | collective-permute-start | bytes 393224 | tf_op jit(solution)/shard_map/ppermute | solution.py:21
  65.9 10.6 %collective-permute-start.11 = (f32[4,64,128]{2,1,0:T(8,128)S(1)}, f32[4,64,128]{2,1,0:T(8,128)S(1)}, u32[]{:S(2)}, u32[]{:S(2)}) collective-permute-start(f32[4,64,128]{2,1,0:T(8,128)S(1)} %get-tuple-element.60), channel_id=1, source_target_pairs={{0,8},{8,16},{16,24},{24,32},{32,40},{40,48},{48,56},{56,64},{64,7... | collective-permute-start | bytes 393224 | tf_op jit(solution)/shard_map/ppermute | solution.py:19
  68.5 32.4 %collective-permute-start.4 = (f32[4,64,128]{2,1,0:T(8,128)}, f32[4,64,128]{2,1,0:T(8,128)S(1)}, u32[]{:S(2)}, u32[]{:S(2)}) collective-permute-start(f32[4,64,128]{2,1,0:T(8,128)} %get-tuple-element.66), channel_id=1, source_target_pairs={{8,0},{16,8},{24,16},{32,24},{40,32},{48,40},{56,48},{64,56},{72,6... | collective-permute-start | bytes 393224 | tf_op jit(solution)/shard_map/ppermute | solution.py:21
  74.5 26.3 %collective-permute-start.5 = (f32[4,64,128]{2,1,0:T(8,128)S(1)}, f32[4,64,128]{2,1,0:T(8,128)S(1)}, u32[]{:S(2)}, u32[]{:S(2)}) collective-permute-start(f32[4,64,128]{2,1,0:T(8,128)S(1)} %get-tuple-element.67), channel_id=1, source_target_pairs={{0,8},{8,16},{16,24},{24,32},{32,40},{40,48},{48,56},{56,64},{64,7... | collective-permute-start | bytes 393224 | tf_op jit(solution)/shard_map/ppermute | solution.py:19
  103.6 9.3 %copy-start.7 = (f32[16,64,128]{2,1,0:T(8,128)}, f32[16,64,128]{2,1,0:T(8,128)S(1)}, u32[]{:S(2)}) copy-start(f32[16,64,128]{2,1,0:T(8,128)S(1)} %get-tuple-element.58) | copy-start | bytes 1572868
  103.6 19.4 %collective-permute-start.12 = (f32[4,64,128]{2,1,0:T(8,128)S(1)}, f32[4,64,128]{2,1,0:T(8,128)S(1)}, u32[]{:S(2)}, u32[]{:S(2)}) collective-permute-start(f32[4,64,128]{2,1,0:T(8,128)S(1)} %get-tuple-element.56), channel_id=1, source_target_pairs={{8,0},{16,8},{24,16},{32,24},{40,32},{48,40},{56,48},{64,56},{72,6... | collective-permute-start | bytes 393224 | tf_op jit(solution)/shard_map/ppermute | solution.py:21
  109.7 13.3 %collective-permute-start.13 = (f32[4,64,128]{2,1,0:T(8,128)S(1)}, f32[4,64,128]{2,1,0:T(8,128)S(1)}, u32[]{:S(2)}, u32[]{:S(2)}) collective-permute-start(f32[4,64,128]{2,1,0:T(8,128)S(1)} %get-tuple-element.57), channel_id=1, source_target_pairs={{0,8},{8,16},{16,24},{24,32},{32,40},{40,48},{48,56},{56,64},{64,7... | collective-permute-start | bytes 393224 | tf_op jit(solution)/shard_map/ppermute | solution.py:19
  114.3 10.7 %copy-start.3 = (f32[16,64,128]{2,1,0:T(8,128)}, f32[16,64,128]{2,1,0:T(8,128)S(1)}, u32[]{:S(2)}) copy-start(f32[16,64,128]{2,1,0:T(8,128)S(1)} %scatter-add.45) | copy-start | bytes 1572868
  114.3 8.7 %copy-start.8 = (f32[16,64,128]{2,1,0:T(8,128)S(1)}, f32[16,64,128]{2,1,0:T(8,128)}, u32[]{:S(2)}) copy-start(f32[16,64,128]{2,1,0:T(8,128)} %copy-done.7) | copy-start | bytes 1572868
  115.0 25.2 %collective-permute-start.6 = (f32[4,64,128]{2,1,0:T(8,128)}, f32[4,64,128]{2,1,0:T(8,128)S(1)}, u32[]{:S(2)}, u32[]{:S(2)}) collective-permute-start(f32[4,64,128]{2,1,0:T(8,128)} %get-tuple-element.64), channel_id=1, source_target_pairs={{8,0},{16,8},{24,16},{32,24},{40,32},{48,40},{56,48},{64,56},{72,6... | collective-permute-start | bytes 393224 | tf_op jit(solution)/shard_map/ppermute | solution.py:21
  121.1 19.2 %collective-permute-start.7 = (f32[4,64,128]{2,1,0:T(8,128)}, f32[4,64,128]{2,1,0:T(8,128)}, u32[]{:S(2)}, u32[]{:S(2)}) collective-permute-start(f32[4,64,128]{2,1,0:T(8,128)} %get-tuple-element.65), channel_id=1, source_target_pairs={{0,8},{8,16},{16,24},{24,32},{32,40},{40,48},{48,56},{56,64},{64,7... | collective-permute-start | bytes 393224 | tf_op jit(solution)/shard_map/ppermute | solution.py:19
  150.8 9.5 %copy-start.4 = (f32[16,64,128]{2,1,0:T(8,128)}, f32[16,64,128]{2,1,0:T(8,128)S(1)}, u32[]{:S(2)}) copy-start(f32[16,64,128]{2,1,0:T(8,128)S(1)} %get-tuple-element.55) | copy-start | bytes 1572868
  150.9 19.6 %collective-permute-start.14 = (f32[4,64,128]{2,1,0:T(8,128)S(1)}, f32[4,64,128]{2,1,0:T(8,128)S(1)}, u32[]{:S(2)}, u32[]{:S(2)}) collective-permute-start(f32[4,64,128]{2,1,0:T(8,128)S(1)} %get-tuple-element.53), channel_id=1, source_target_pairs={{8,0},{16,8},{24,16},{32,24},{40,32},{48,40},{56,48},{64,56},{72,6... | collective-permute-start | bytes 393224 | tf_op jit(solution)/shard_map/ppermute | solution.py:21
  156.9 13.5 %collective-permute-start.15 = (f32[4,64,128]{2,1,0:T(8,128)S(1)}, f32[4,64,128]{2,1,0:T(8,128)}, u32[]{:S(2)}, u32[]{:S(2)}) collective-permute-start(f32[4,64,128]{2,1,0:T(8,128)S(1)} %get-tuple-element.54), channel_id=1, source_target_pairs={{0,8},{8,16},{16,24},{24,32},{32,40},{40,48},{48,56},{56,64},{64,7... | collective-permute-start | bytes 393224 | tf_op jit(solution)/shard_map/ppermute | solution.py:19
  161.7 8.7 %copy-start.5 = (f32[16,64,128]{2,1,0:T(8,128)S(1)}, f32[16,64,128]{2,1,0:T(8,128)}, u32[]{:S(2)}) copy-start(f32[16,64,128]{2,1,0:T(8,128)} %copy-done.4) | copy-start | bytes 1572868
  162.4 25.5 %collective-permute-start.8 = (f32[4,64,128]{2,1,0:T(8,128)}, f32[4,64,128]{2,1,0:T(8,128)S(1)}, u32[]{:S(2)}, u32[]{:S(2)}) collective-permute-start(f32[4,64,128]{2,1,0:T(8,128)} %get-tuple-element.62), channel_id=1, source_target_pairs={{8,0},{16,8},{24,16},{32,24},{40,32},{48,40},{56,48},{64,56},{72,6... | collective-permute-start | bytes 393224 | tf_op jit(solution)/shard_map/ppermute | solution.py:21
  168.5 19.4 %collective-permute-start.9 = (f32[4,64,128]{2,1,0:T(8,128)}, f32[4,64,128]{2,1,0:T(8,128)S(1)}, u32[]{:S(2)}, u32[]{:S(2)}) collective-permute-start(f32[4,64,128]{2,1,0:T(8,128)} %get-tuple-element.63), channel_id=1, source_target_pairs={{0,8},{8,16},{16,24},{24,32},{32,40},{40,48},{48,56},{56,64},{64,7... | collective-permute-start | bytes 393224 | tf_op jit(solution)/shard_map/ppermute | solution.py:19
  244.6 111.4 %copy-start.12 = (f32[16,8,128]{2,1,0:T(8,128)}, f32[16,8,128]{2,1,0:T(8,128)S(1)}, u32[]{:S(2)}) copy-start(f32[16,8,128]{2,1,0:T(8,128)S(1)} %broadcast_multiply_fusion) | copy-start | bytes 196612
  244.6 115.1 %copy-start.9 = (f32[2,5,16,8,128]{4,3,2,1,0:T(8,128)S(1)}, f32[2,5,16,8,128]{4,3,2,1,0:T(8,128)}, u32[]{:S(2)}) copy-start(f32[2,5,16,8,128]{4,3,2,1,0:T(8,128)} %param.25) | copy-start | bytes 1966084
  244.6 115.1 %copy-start.11 = (f32[16,8,128]{2,1,0:T(8,128)S(1)}, f32[16,8,128]{2,1,0:T(8,128)}, u32[]{:S(2)}) copy-start(f32[16,8,128]{2,1,0:T(8,128)} %reduce-scatter.2.cloned.1.call-done) | copy-start | bytes 196612
Sparse Core Ops, SparseCore 0:
  192.0 51.6 reduce-scatter.1
